TPU v7x, 32 devices: a whole 2x2x4 slice. The times are simulated.
32 devices in a mesh: tm: 4 (over y, x), res: 8 (over z, core).
Axes of the slice: x: 2, y: 2, z: 4, core: 2. Of those that a mesh axis runs over, the one named last changes fastest.
Arguments:
- node_feats: bfloat16 [4, 1024, 512], P('tm', 'res'), may hold values from -6 to 6
- edge_feats: bfloat16 [4, 1024, 60, 192], P('tm', 'res'), may hold values from -6 to 6
- node_cotan: bfloat16 [4, 1024, 512], P('tm', 'res'), may hold values from -6 to 6
- edge_cotan: bfloat16 [4, 1024, 60, 192], P('tm', 'res'), may hold values from -6 to 6
- neighbour: int32 [1024, 60], P('res'), may hold values from 0 to 383, as said below
- edge_mask: int32 [1024, 60], P('res'), may hold values from 0 to 1, as said below
- fetch_rows: int32 [8, 8, 32], P('res'), may hold values from 0 to 1023, as said below
- chain_ids: int32 [1024], P('res'), may hold values from 0 to 23, as said below
- complex_flag: int32 [1024], P('res'), may hold values from 0 to 1, as said below
- message_in: bfloat16 [1216, 512], replicated, may hold values from -0.15625 to 0.15625
- message_mid: bfloat16 [512, 512], replicated, may hold values from -0.25 to 0.25
- message_out: bfloat16 [512, 512], replicated, may hold values from -0.75 to 0.75
- gain_node: bfloat16 [512], replicated, may hold values from 0.5 to 1.5
- offset_node: bfloat16 [512], replicated, may hold values from -3 to 3
- expand_weight: bfloat16 [512, 2048], replicated, may hold values from -0.25 to 0.25
- contract_weight: bfloat16 [2048, 512], replicated, may hold values from -0.125 to 0.125
- gain_ffn: bfloat16 [512], replicated, may hold values from 0.5 to 1.5
- offset_ffn: bfloat16 [512], replicated, may hold values from -3 to 3
- update_in: bfloat16 [1216, 192], replicated, may hold values from -0.15625 to 0.15625
- update_mid: bfloat16 [192, 192], replicated, may hold values from -0.4375 to 0.4375
- update_out: bfloat16 [192, 192], replicated, may hold values from -0.4375 to 0.4375
- gain_edge: bfloat16 [192], replicated, may hold values from 0.5 to 1.5
- offset_edge: bfloat16 [192], replicated, may hold values from -3 to 3
Outputs:
- node_out: bfloat16 [4, 1024, 512], P('tm', 'res')
- edge_out: bfloat16 [4, 1024, 60, 192], P('tm', 'res')
- node_grad: float32 [4, 1024, 512], P('tm', 'res')
- edge_grad: float32 [4, 1024, 60, 192], P('tm', 'res')
- grad_message_in: float32 [1216, 512], replicated
- grad_message_mid: float32 [512, 512], replicated
- grad_message_out: float32 [512, 512], replicated
- grad_gain_node: float32 [512], replicated
- grad_offset_node: float32 [512], replicated
- grad_expand: float32 [512, 2048], replicated
- grad_contract: float32 [2048, 512], replicated
- grad_gain_ffn: float32 [512], replicated
- grad_offset_ffn: float32 [512], replicated
- grad_update_in: float32 [1216, 192], replicated
- grad_update_mid: float32 [192, 192], replicated
- grad_update_out: float32 [192, 192], replicated
- grad_gain_edge: float32 [192], replicated
- grad_offset_edge: float32 [192], replicated
Inputs may be any that keep to these rules, and one draw needn't show every extreme that they name: `neighbour`: below 128 an entry names a residue of the own block; an entry s of 128 or more names the residue fetch_rows[block, (s - 128) // 32, (s - 128) % 32]. fetch_rows[d, p] holds 32 distinct residues of block p, that is of p * 128 to (p + 1) * 128 - 1. `chain_ids`: never falls along residues; no chain crosses from one block of 128 residues to the next. `complex_flag`: equal for all residues of a chain; the first chain of every block is in the complex. `edge_mask`: some residues are padding with no live edge.
All inputs are finite; a program needn't handle non-finite values.
Results may differ from a plain program's by a relative error of at most 0.02.
Values may be sent and summed in bfloat16 or wider, within the bound.
A program may use at most 256 MiB of HBM per device.

v0:
```python
import jax
import jax.numpy as jnp
from jax import lax
from jax.sharding import PartitionSpec as P

EPSILON = 1e-05


def activate(values):
    return jax.nn.gelu(values, approximate=True)


def layer_norm(values, gain_vec, offset):
    centred = values - jnp.mean(values, axis=-1, keepdims=True)
    spread = jnp.mean(centred * centred, axis=-1, keepdims=True)
    return centred * lax.rsqrt(spread + EPSILON) * gain_vec + offset


def forward_dot(left_op, right_op):
    return jnp.dot(left_op, right_op, preferred_element_type=jnp.float32)


def weight_grad(inputs, grad_rows):
    return lax.dot_general(
        inputs, grad_rows, (((0,), (0,)), ((), ())), preferred_element_type=jnp.float32
    )


def input_grad(grad_rows, weight):
    return lax.dot_general(
        grad_rows, weight, (((1,), (1,)), ((), ())), preferred_element_type=jnp.float32
    )


def edge_dot(edges, weight):
    return jnp.einsum("rke,ef->rkf", edges, weight, preferred_element_type=jnp.float32)


def edge_weight_grad(edges, grads):
    return jnp.einsum("rke,rkf->ef", edges, grads, preferred_element_type=jnp.float32)


def edge_input_grad(grads, weight):
    return jnp.einsum("rkf,ef->rke", grads, weight, preferred_element_type=jnp.float32)


def through_gate(pre_act, grad_out):
    unused, pullback = jax.vjp(activate, pre_act)
    return pullback(grad_out)[0].astype(jnp.bfloat16)


def one_hot_rows(indices, table_len):
    return (indices[:, None] == jnp.arange(table_len, dtype=jnp.int32)[None, :]).astype(
        jnp.bfloat16
    )


def pick_rows(picker, table):
    upper = table.astype(jnp.bfloat16)
    lower = (table - upper.astype(jnp.float32)).astype(jnp.bfloat16)
    return jnp.einsum(
        "rkl,ld->rkd", picker, upper, preferred_element_type=jnp.float32
    ) + jnp.einsum("rkl,ld->rkd", picker, lower, preferred_element_type=jnp.float32)


def table_grad(picker, grads):
    return jnp.einsum("rkl,rkd->ld", picker, grads, preferred_element_type=jnp.float32)


def message_pass(self_proj, table_proj, picker, edge_in, edge_weight, mid_weight, out_weight):
    gathered = pick_rows(picker, table_proj)
    pre_one = self_proj[:, None, :] + gathered + edge_dot(edge_in, edge_weight)
    hidden_one = activate(pre_one).astype(jnp.bfloat16)
    pre_two = edge_dot(hidden_one, mid_weight)
    hidden_two = activate(pre_two).astype(jnp.bfloat16)
    return (pre_one, hidden_one, pre_two, hidden_two, edge_dot(hidden_two, out_weight))


def local(
    node_feats,
    edge_feats,
    node_cotan,
    edge_cotan,
    neighbour,
    edge_mask,
    fetch_rows,
    chain_ids,
    complex_flag,
    message_in,
    message_mid,
    message_out,
    gain_node,
    offset_node,
    expand_weight,
    contract_weight,
    gain_ffn,
    offset_ffn,
    update_in,
    update_mid,
    update_out,
    gain_edge,
    offset_edge,
):
    row_count, fanout = neighbour.shape
    feat_width = node_feats.shape[2]
    peer_count = fetch_rows.shape[1]
    slot_count = fetch_rows.shape[2]
    table_len = row_count + peer_count * slot_count
    node_in = node_feats[0]
    edge_in = edge_feats[0]
    wanted = fetch_rows[0].reshape(peer_count * slot_count)
    my_index = lax.axis_index("res")
    own_ids = my_index * row_count + jnp.arange(row_count, dtype=jnp.int32)
    table_ids = jnp.concatenate([own_ids, wanted], axis=0)
    tag_local = chain_ids * 2 + complex_flag
    picker = (
        neighbour[:, :, None] == jnp.arange(table_len, dtype=jnp.int32)[None, None, :]
    ).astype(jnp.bfloat16)
    all_rows, all_tags = (
        lax.all_gather(node_in, "res", axis=0, tiled=True),
        lax.all_gather(tag_local, "res", axis=0, tiled=True),
    )
    wanted_picker = one_hot_rows(wanted, peer_count * row_count)
    far_rows = forward_dot(wanted_picker, all_rows).astype(jnp.bfloat16)
    far_tags = jnp.take(all_tags, wanted)
    table_rows = jnp.concatenate([node_in, far_rows], axis=0)
    table_tags = jnp.concatenate([tag_local, far_tags], axis=0)
    other_tag = jnp.take(table_tags, neighbour, axis=0)
    joined = jnp.logical_or(
        chain_ids[:, None] == other_tag // 2, complex_flag[:, None] * (other_tag % 2) > 0
    )
    keep = edge_mask.astype(jnp.float32) * joined.astype(jnp.float32)
    counted = jnp.maximum(jnp.sum(keep, axis=1), 1.0)
    self_weight = message_in[:feat_width]
    neigh_weight = message_in[feat_width : 2 * feat_width]
    message_edge = message_in[2 * feat_width :]
    self_proj = forward_dot(node_in, self_weight)
    table_proj = forward_dot(table_rows, neigh_weight)
    kept = message_pass(
        self_proj, table_proj, picker, edge_in, message_edge, message_mid, message_out
    )
    aggregate = jnp.sum(kept[4] * keep[:, :, None], axis=1) / counted[:, None]
    first, first_pull = jax.vjp(
        layer_norm,
        node_in.astype(jnp.float32) + aggregate,
        gain_node.astype(jnp.float32),
        offset_node.astype(jnp.float32),
    )
    first_low = first.astype(jnp.bfloat16)
    inner = forward_dot(first_low, expand_weight)
    acted = activate(inner).astype(jnp.bfloat16)
    ffn_out = forward_dot(acted, contract_weight)
    updated, second_pull = jax.vjp(
        layer_norm, first + ffn_out, gain_ffn.astype(jnp.float32), offset_ffn.astype(jnp.float32)
    )
    updated_low = updated.astype(jnp.bfloat16)
    far_new = forward_dot(
        wanted_picker, lax.all_gather(updated_low, "res", axis=0, tiled=True)
    ).astype(jnp.bfloat16)
    table_new = jnp.concatenate([updated_low, far_new], axis=0)
    update_self = update_in[:feat_width]
    update_neigh = update_in[feat_width : 2 * feat_width]
    update_edge = update_in[2 * feat_width :]
    self_edge = forward_dot(updated_low, update_self)
    table_edge = forward_dot(table_new, update_neigh)
    gathered_edge = pick_rows(picker, table_edge)
    pre_three = self_edge[:, None, :] + gathered_edge + edge_dot(edge_in, update_edge)
    hidden_three = activate(pre_three).astype(jnp.bfloat16)
    pre_four = edge_dot(hidden_three, update_mid)
    hidden_four = activate(pre_four).astype(jnp.bfloat16)
    branch = edge_dot(hidden_four, update_out)
    edge_new, third_pull = jax.vjp(
        layer_norm,
        edge_in.astype(jnp.float32) + branch,
        gain_edge.astype(jnp.float32),
        offset_edge.astype(jnp.float32),
    )
    delta_resid, grad_gain_edge, grad_offset_edge = third_pull(edge_cotan[0].astype(jnp.float32))
    delta_branch = delta_resid.astype(jnp.bfloat16)
    grad_update_out = edge_weight_grad(hidden_four, delta_branch)
    delta_four = through_gate(pre_four, edge_input_grad(delta_branch, update_out))
    grad_update_mid = edge_weight_grad(hidden_three, delta_four)
    delta_three = through_gate(pre_three, edge_input_grad(delta_four, update_mid))
    grad_update_edge = edge_weight_grad(edge_in, delta_three)
    delta_edge_in = delta_resid + edge_input_grad(delta_three, update_edge)
    delta_self_edge = jnp.sum(delta_three, axis=1, dtype=jnp.float32).astype(jnp.bfloat16)
    delta_table_edge = table_grad(picker, delta_three)
    table_picker = one_hot_rows(table_ids, peer_count * row_count).astype(jnp.float32)
    spread_edge = lax.dot_general(
        table_picker, delta_table_edge, (((0,), (0,)), ((), ())), precision=lax.Precision.HIGHEST
    )
    own_edge = lax.psum_scatter(
        spread_edge.astype(jnp.bfloat16), "res", scatter_dimension=0, tiled=True
    )
    grad_update_self = weight_grad(updated_low, delta_self_edge)
    grad_update_neigh = weight_grad(updated_low, own_edge)
    delta_updated = (
        node_cotan[0].astype(jnp.float32)
        + input_grad(delta_self_edge, update_self)
        + input_grad(own_edge, update_neigh)
    )
    delta_second, grad_gain_ffn, grad_offset_ffn = second_pull(delta_updated)
    delta_ffn = delta_second.astype(jnp.bfloat16)
    grad_contract = weight_grad(acted, delta_ffn)
    delta_inner = through_gate(inner, input_grad(delta_ffn, contract_weight))
    grad_expand = weight_grad(first_low, delta_inner)
    delta_first = delta_second + input_grad(delta_inner, expand_weight)
    delta_first_in, grad_gain_node, grad_offset_node = first_pull(delta_first)
    delta_message = ((delta_first_in / counted[:, None])[:, None, :] * keep[:, :, None]).astype(
        jnp.bfloat16
    )
    pre_one, hidden_one, pre_two, hidden_two, unused_message = kept
    grad_message_out = edge_weight_grad(hidden_two, delta_message)
    delta_two = through_gate(pre_two, edge_input_grad(delta_message, message_out))
    grad_message_mid = edge_weight_grad(hidden_one, delta_two)
    delta_one = through_gate(pre_one, edge_input_grad(delta_two, message_mid))
    grad_message_edge = edge_weight_grad(edge_in, delta_one)
    delta_edge_in = delta_edge_in + edge_input_grad(delta_one, message_edge)
    delta_self = jnp.sum(delta_one, axis=1, dtype=jnp.float32).astype(jnp.bfloat16)
    delta_table = table_grad(picker, delta_one)
    spread_node = lax.dot_general(
        table_picker, delta_table, (((0,), (0,)), ((), ())), precision=lax.Precision.HIGHEST
    )
    own_node = lax.psum_scatter(
        spread_node.astype(jnp.bfloat16), "res", scatter_dimension=0, tiled=True
    )
    grad_message_self = weight_grad(node_in, delta_self)
    grad_message_neigh = weight_grad(node_in, own_node)
    delta_node_in = (
        delta_first_in + input_grad(delta_self, self_weight) + input_grad(own_node, neigh_weight)
    )
    grad_message_in = jnp.concatenate(
        [grad_message_self, grad_message_neigh, grad_message_edge], axis=0
    )
    grad_update_in = jnp.concatenate(
        [grad_update_self, grad_update_neigh, grad_update_edge], axis=0
    )
    totals = lax.psum(
        (
            grad_message_in,
            grad_message_mid,
            grad_message_out,
            grad_gain_node,
            grad_offset_node,
            grad_expand,
            grad_contract,
            grad_gain_ffn,
            grad_offset_ffn,
            grad_update_in,
            grad_update_mid,
            grad_update_out,
            grad_gain_edge,
            grad_offset_edge,
        ),
        ("tm", "res"),
    )
    return (
        updated_low[None],
        edge_new.astype(jnp.bfloat16)[None],
        delta_node_in[None],
        delta_edge_in[None],
        totals[0],
        totals[1],
        totals[2],
        totals[3],
        totals[4],
        totals[5],
        totals[6],
        totals[7],
        totals[8],
        totals[9],
        totals[10],
        totals[11],
        totals[12],
        totals[13],
    )


def solution(mesh):
    placed = (
        P("tm", "res", None),
        P("tm", "res", None, None),
        P("tm", "res", None),
        P("tm", "res", None, None),
        P("res", None),
        P("res", None),
        P("res", None, None),
        P("res"),
        P("res"),
        P(),
        P(),
        P(),
        P(),
        P(),
        P(),
        P(),
        P(),
        P(),
        P(),
        P(),
        P(),
        P(),
        P(),
    )
    return jax.shard_map(
        local,
        mesh=mesh,
        in_specs=placed,
        out_specs=(
            P("tm", "res", None),
            P("tm", "res", None, None),
            P("tm", "res", None),
            P("tm", "res", None, None),
            P(),
            P(),
            P(),
            P(),
            P(),
            P(),
            P(),
            P(),
            P(),
            P(),
            P(),
            P(),
            P(),
            P(),
        ),
        check_vma=False,
    )
```

profile of v0, /device:TPU:0, one launch (start us, length us, event | category | flops | bytes accessed | tf_op | source)
XLA Modules:
  0.0 621.4 jit_solution(12304324607836840426)
XLA Ops:
  13.0 13.4 %all-gather.1 = s32[8,1,128]{2,1,0:T(1,128)S(1)} all-gather(s32[1,1,128]{2,1,0:T(1,128)S(1)} %bitcast.183), channel_id=1, replica_groups=mesh['tm'=4,'res'=8] {'res'}, dimensions={0}, use_global_device_ids=true | all-gather | bytes 4608 | tf_op jit(solution)/shard_map/all_gather | solution.py:121
  26.3 0.9 copy.58
  27.3 1.4 gather_fusion
  28.8 45.2 %gather_fusion.1 = s32[7680]{0:T(1024)S(1)} fusion(s32[384]{0:T(512)S(1)} %pad_add_fusion, s32[8192]{0:T(1024)S(1)} %pad_clamp_fusion), kind=kCustom, calls=%fused_computation.1 | custom fusion | bytes 92160 | tf_op jit(solution)/shard_map/jit(_take)/gather | solution.py:128
  74.6 1.3 fusion.97
  75.8 9.6 %fusion.58 = f32[128,60,512]{2,0,1:T(8,128)} fusion(bf16[1,128,60,192]{1,3,2,0:T(8,128)(2,1)} %param.24, bf16[1216,512]{1,0:T(8,128)(2,1)} %param.32), kind=kOutput, calls=%fused_computation.85 | convolution fusion | flops 1509949440 | bytes 18874368 | tf_op jit(solution)/shard_map/rke,ef->rkf/dot_general | solution.py:36
  85.4 1.7 convolution_convert_fusion.1
  87.2 1.4 fusion.94
  88.6 7.7 %fusion.18 = f32[128,60,512]{2,0,1:T(8,128)} fusion(s32[128,60]{0,1:T(8,128)S(1)} %copy-done.24, f32[384,512]{1,0:T(8,128)S(1)} %fusion.94), kind=kOutput, calls=%fused_computation.30 | convolution fusion | flops 3023634432 | bytes 16545792 | tf_op jit(solution)/shard_map/rkl,ld->rkd/dot_general | solution.py:63
  96.3 17.7 %add_add_fusion = f32[128,60,512]{2,0,1:T(8,128)} fusion(f32[128,60,512]{2,0,1:T(8,128)} %fusion.58, f32[128,60,512]{2,0,1:T(8,128)} %fusion.18, f32[128,512]{1,0:T(8,128)S(1)} %fusion.97, s32[128,60]{0,1:T(8,128)S(1)} %copy-done.24, f32[384,512]{1,0:T(8,128)S(1)} %fusion.94), kind=kOutput, calls=%fused_computation.24 | convolution fusion | flops 3034841088 | bytes 48265216 | tf_op jit(solution)/shard_map/rkl,ld->rkd/dot_general | solution.py:61
  114.0 16.2 %multiply_convert_fusion.1 = (bf16[128,60,512]{2,0,1:T(8,128)(2,1)S(1)}, f32[128,60,512]{2,0,1:T(8,128)}) fusion(bf16[512,512]{1,0:T(8,128)(2,1)} %param.33, f32[128,60,512]{2,0,1:T(8,128)} %add_add_fusion), kind=kOutput, calls=%fused_computation.22 | convolution fusion | flops 4097310720 | bytes 39845888 | tf_op jit(solution)/shard_map/rke,ef->rkf/dot_general | solution.py:36
  130.2 4.5 multiply_reduce_fusion
  135.7 1.0 copy-done.12
  137.6 0.8 add_convert_fusion.4
  138.6 1.1 fusion.118
  139.7 19.2 %all-gather.5.cloned.1.call-done = bf16[1024,512]{1,0:T(8,128)(2,1)} async-done(((bf16[128,512]{1,0:T(8,128)(2,1)}), bf16[1024,512]{1,0:T(8,128)(2,1)}) %all-gather.5.cloned.1.call-update) | async-done | bytes 1048592 | tf_op jit(solution)/shard_map/all_gather | solution.py:158
  158.9 1.7 convolution_convert_fusion
  160.6 1.2 fusion.104
  161.8 2.7 fusion.16
  164.5 2.4 fusion.17
  167.0 1.5 add_add_fusion.2
  168.5 3.3 fusion.128
  171.9 3.1 fusion.161
  175.0 2.5 fusion.29
  177.6 6.6 %fusion.30 = (f32[192]{0:T(256)}, f32[128,60]{0,1:T(8,128)S(1)}, bf16[1,128,60,192]{1,3,2,0:T(8,128)(2,1)}) fusion(bf16[1,128,60,192]{1,3,2,0:T(8,128)(2,1)S(1)} %copy-done.3, f32[128,60,192]{0,2,1:T(8,128)S(1)} %get-tuple-element.58, f32[128,60]{0,1:T(8,128)S(1)} %get-tuple-element.52, f32[128,60]{0,1:T(8,128)S(1)} %broadcast_multiply_fusion, ...), kind=kLoop, calls=%fused_computation.49 | loop fusion | flops 20635968 | bytes 11921664 | tf_op jit(solution)/shard_map/transpose(jvp())/reduce_sum | solution.py:16
  184.2 4.3 convolution_bitcast_fusion.3
  188.6 6.4 %fusion.44 = bf16[128,60,192]{0,2,1:T(8,128)(2,1)S(1)} fusion(f32[128,60,192]{0,2,1:T(8,128)S(1)} %fusion.128, f32[128,60]{0,1:T(8,128)S(1)} %negate_multiply_fusion, bf16[192,192]{1,0:T(8,128)(2,1)S(1)} %copy-done.87, bf16[1,128,60,192]{1,3,2,0:T(8,128)(2,1)S(1)} %copy-done.3, f32[128,60,192]{0,2,1:T(8,128)S(1)} %get-tuple-element.58, ...), kind=kOutput, calls=%fused_computation.63 | convolution fusion | flops 608993280 | bytes 17892096 | tf_op jit(solution)/shard_map/rkf,ef->rke/dot_general | solution.py:44
  195.0 5.0 fusion.162
  200.0 1.6 fusion.73
  201.7 2.3 fusion.71
  204.0 1.7 fusion.67
  205.8 2.0 copy.84
  207.8 1.1 convolution_add_fusion.4
  209.0 0.9 fusion.164
  209.9 6.2 %convolution_bitcast_fusion.4 = f32[192,192]{1,0:T(8,128)} fusion(bf16[128,60,192]{0,2,1:T(8,128)(2,1)} %copy-done.92, f32[128,60,192]{0,2,1:T(8,128)} %copy-done.9), kind=kOutput, calls=%fused_computation.113 | convolution fusion | flops 579502080 | bytes 8994816 | tf_op jit(solution)/shard_map/rke,rkf->ef/dot_general | solution.py:40
  216.2 22.4 %reduce-scatter.7.cloned.1.call-done = bf16[128,192]{1,0:T(8,128)(2,1)} async-done(((bf16[1024,192]{1,0:T(8,128)(2,1)}), bf16[128,192]{1,0:T(8,128)(2,1)}) %reduce-scatter.7.cloned.1.call-update) | async-done | bytes 49168
  238.6 1.7 multiply_reduce_fusion.2
  240.6 2.9 fusion.82
  243.5 1.5 multiply_reduce_fusion.3
  245.4 8.7 %fusion.65 = f32[512,512]{1,0:T(8,128)} fusion(bf16[128,60,512]{2,0,1:T(8,128)(2,1)} %copy-done.91, f32[128,512]{1,0:T(8,128)S(1)} %add_divide_fusion, f32[128,60]{0,1:T(8,128)S(1)} %copy-done.49), kind=kOutput, calls=%fused_computation.94 | convolution fusion | flops 4034396160 | bytes 9205760 | tf_op jit(solution)/shard_map/rke,rkf->ef/dot_general | solution.py:40
  254.1 17.7 %fusion.13 = bf16[128,60,512]{2,0,1:T(8,128)(2,1)} fusion(f32[128,60,512]{2,0,1:T(8,128)} %get-tuple-element.54, f32[128,512]{1,0:T(8,128)S(1)} %add_divide_fusion, f32[128,60]{0,1:T(8,128)S(1)} %copy-done.49, bf16[512,512]{1,0:T(8,128)(2,1)S(1)} %copy-done.85), kind=kOutput, calls=%fused_computation.19 | convolution fusion | flops 4113039360 | bytes 24410112 | tf_op jit(solution)/shard_map/rkf,ef->rke/dot_general | solution.py:44
  271.9 15.9 %fusion.163 = (bf16[128,512]{1,0:T(8,128)(2,1)S(1)}, bf16[128,60,512]{2,0,1:T(8,128)(2,1)S(1)}) fusion(f32[128,60,512]{2,0,1:T(8,128)S(1)} %bitcast.180, bf16[128,60,512]{2,0,1:T(8,128)(2,1)} %fusion.13, bf16[512,512]{1,0:T(8,128)(2,1)S(1)} %copy-done.86), kind=kOutput, calls=%fused_computation.246 | convolution fusion | flops 4109041664 | bytes 32112640 | tf_op jit(solution)/shard_map/rkf,ef->rke/dot_general | solution.py:44
  287.9 6.5 %fusion.68 = f32[192,512]{1,0:T(8,128)} fusion(bf16[128,60,512]{2,0,1:T(8,128)(2,1)S(1)} %get-tuple-element.64, bf16[1,128,60,192]{1,3,2,0:T(8,128)(2,1)} %param.24), kind=kOutput, calls=%fused_computation.100 | convolution fusion | flops 1509949440 | bytes 11206656 | tf_op jit(solution)/shard_map/rke,rkf->ef/dot_general | solution.py:40
  294.4 3.2 fusion.66
  297.6 2.8 fusion.149
  300.4 2.8 fusion.151
  303.3 2.9 fusion.64
  306.9 1.0 pad_maximum_fusion.1
  307.9 12.3 %convolution_bitcast_fusion = f32[512,512]{1,0:T(8,128)} fusion(bf16[128,60,512]{2,0,1:T(8,128)(2,1)} %fusion.13, f32[128,60,512]{2,0,1:T(8,128)} %add_add_fusion), kind=kOutput, calls=%fused_computation.95 | convolution fusion | flops 4061921280 | bytes 24641536 | tf_op jit(solution)/shard_map/rke,rkf->ef/dot_general | solution.py:40
  320.2 16.6 %reduce-scatter.5.cloned.1.call-done = bf16[128,512]{1,0:T(8,128)(2,1)} async-done(((bf16[1024,512]{1,0:T(8,128)(2,1)}), bf16[128,512]{1,0:T(8,128)(2,1)}) %reduce-scatter.5.cloned.1.call-update) | async-done | bytes 131088 | tf_op jit(solution)/shard_map/reduce_scatter | solution.py:224
  336.7 1.2 convolution_bitcast_fusion.1
  338.0 1.7 pad_maximum_fusion
  339.8 2.5 convert_reduce_fusion
  343.1 40.1 %all-reduce = (f32[512]{0:T(512)}, f32[512]{0:T(512)}, f32[512]{0:T(512)}, f32[512]{0:T(512)}, f32[192]{0:T(256)}, /*index=5*/f32[192]{0:T(256)}) all-reduce(f32[512]{0:T(512)S(1)} %copy-done.66, f32[512]{0:T(512)S(1)} %copy-done.67, f32[512]{0:T(512)S(1)} %copy-done.64, ...), channel_id=1, replica_groups=mesh['tm'=4,'res'=8] {'tm','res'}, use_global_device_ids=true, to_apply=%region_22.23 | all-reduce | flops 2432 | bytes 19456 | tf_op jit(solution)/shard_map/psum | solution.py:238
  383.6 5.4 fusion.110
  389.5 6.5 %add_bitcast_fusion = f32[1,128,60,192]{1,3,2,0:T(8,128)} fusion(f32[128,60,192]{0,2,1:T(8,128)S(1)} %fusion.110, f32[128,60]{0,1:T(8,128)S(1)} %copy-done.41, bf16[128,60,192]{0,2,1:T(8,128)(2,1)S(1)} %copy-done.19, bf16[1216,192]{0,1:T(8,128)(2,1)} %param.41, f32[128,60]{0,1:T(8,128)S(1)} %copy-done.33, f32[128,60,192]{0,2,1:T(8,128)} %copy-done.2, ...), kind=kOutput, calls=%fused_computation.64 | convolution fusion | flops 580976640 | bytes 23814912 | tf_op jit(solution)/shard_map/rkf,ef->rke/dot_general | solution.py:44
  396.0 1.0 fusion.72
  397.1 204.0 %all-reduce.4.cloned.1.call-done = (f32[1216,512]{1,0:T(8,128)}, f32[512,512]{1,0:T(8,128)}, f32[512,512]{1,0:T(8,128)}, f32[512,2048]{1,0:T(8,128)}, f32[2048,5...) async-done(((f32[1216,512]{1,0:T(8,128)}, f32[512,512]{1,0:T(8,128)}, f32[512,512]{1,0:T(8,128)}, f32[512,2048]{1,0:T(8,128)}, ...) | async-done | bytes 14204944 | tf_op jit(solution)/shard_map/psum | solution.py:238
  601.1 3.5 copy.94
  604.6 2.4 copy.95
  607.0 1.0 copy.96
  608.0 2.1 copy.97
  610.1 2.0 copy.98
  612.1 0.9 copy.99
  (253 shorter events, 12.7 us)
Async XLA Ops:
  7.2 128.0 %copy-start = (bf16[512,2048]{1,0:T(8,128)(2,1)S(1)}, bf16[512,2048]{1,0:T(8,128)(2,1)}, u32[]{:S(2)}) copy-start(bf16[512,2048]{1,0:T(8,128)(2,1)} %param.37) | copy-start | bytes 6291460
  7.2 78.2 %all-gather.7.cloned.1.call-start = ((), (), s32[]{:S(2)}) async-start(), calls=%async_computation.4 | async-start | bytes 1179648 | tf_op jit(solution)/shard_map/all_gather | solution.py:120
  7.9 150.9 %all-gather.5.cloned.1.call-start = ((), (), s32[]{:S(2)}) async-start(), calls=%async_computation.2 | async-start | bytes 1179648 | tf_op jit(solution)/shard_map/all_gather | solution.py:158
  10.2 125.5 %copy-start.45 = (f32[512]{0:T(512)}, f32[512]{0:T(512)S(1)}, u32[]{:S(2)}) copy-start(f32[512]{0:T(512)S(1)} %convert_element_type.134) | copy-start | bytes 6148
  10.9 126.7 %copy-start.42 = (f32[512]{0:T(512)}, f32[512]{0:T(512)S(1)}, u32[]{:S(2)}) copy-start(f32[512]{0:T(512)S(1)} %convert_element_type.138) | copy-start | bytes 6148
  11.6 124.1 %copy-start.52 = (f32[512]{0:T(512)}, f32[512]{0:T(512)S(1)}, u32[]{:S(2)}) copy-start(f32[512]{0:T(512)S(1)} %convert_element_type.135) | copy-start | bytes 6148
  12.3 125.3 %copy-start.50 = (f32[512]{0:T(512)}, f32[512]{0:T(512)S(1)}, u32[]{:S(2)}) copy-start(f32[512]{0:T(512)S(1)} %convert_element_type.139) | copy-start | bytes 6148
  28.7 45.4 %copy-start.47 = (s32[128,60]{0,1:T(8,128)S(1)}, s32[128,60]{0,1:T(8,128)}, u32[]{:S(2)}) copy-start(s32[128,60]{0,1:T(8,128)} %param.28) | copy-start | bytes 92164
  28.7 45.5 %copy-start.77 = (s32[128]{0:T(128)S(1)}, s32[128]{0:T(128)}, u32[]{:S(2)}) copy-start(s32[128]{0:T(128)} %param.31) | copy-start | bytes 1540
  28.7 45.5 %copy-start.78 = (s32[128]{0:T(128)S(1)}, s32[128]{0:T(128)}, u32[]{:S(2)}) copy-start(s32[128]{0:T(128)} %param.30) | copy-start | bytes 1540
  28.8 45.8 %copy-start.14 = (bf16[1,128,512]{2,1,0:T(8,128)(2,1)S(1)}, bf16[1,128,512]{2,1,0:T(8,128)(2,1)}, u32[]{:S(2)}) copy-start(bf16[1,128,512]{2,1,0:T(8,128)(2,1)} %param.23) | copy-start | bytes 393220
  74.5 55.7 %copy-start.48 = (f32[128,60]{0,1:T(8,128)}, f32[128,60]{0,1:T(8,128)S(1)}, u32[]{:S(2)}) copy-start(f32[128,60]{0,1:T(8,128)S(1)} %copy.62) | copy-start | bytes 92164
  74.6 60.2 %copy-start.73 = (f32[128]{0:T(128)}, f32[128]{0:T(128)S(1)}, u32[]{:S(2)}) copy-start(f32[128]{0:T(128)S(1)} %broadcast_maximum_fusion) | copy-start | bytes 1540
  75.8 12.7 %copy-start.24 = (s32[128,60]{0,1:T(8,128)S(1)}, s32[128,60]{0,1:T(8,128)}, u32[]{:S(2)}) copy-start(s32[128,60]{0,1:T(8,128)} %param.27) | copy-start | bytes 92164
  114.0 16.2 %copy-start.84 = (bf16[512,512]{1,0:T(8,128)(2,1)S(1)}, bf16[512,512]{1,0:T(8,128)(2,1)}, u32[]{:S(2)}) copy-start(bf16[512,512]{1,0:T(8,128)(2,1)} %param.34) | copy-start | bytes 1572868
  130.2 6.5 %copy-start.83 = (bf16[2048,512]{1,0:T(8,128)(2,1)S(1)}, bf16[2048,512]{1,0:T(8,128)(2,1)}, u32[]{:S(2)}) copy-start(bf16[2048,512]{1,0:T(8,128)(2,1)} %param.38) | copy-start | bytes 6291460
  135.2 26.7 %copy-start.79 = (f32[128]{0:T(128)}, f32[128]{0:T(128)S(1)}, u32[]{:S(2)}) copy-start(f32[128]{0:T(128)S(1)} %multiply_reduce_fusion.7) | copy-start | bytes 1540
  135.2 26.6 %copy-start.68 = (f32[128]{0:T(128)}, f32[128]{0:T(128)S(1)}, u32[]{:S(2)}) copy-start(f32[128]{0:T(128)S(1)} %fusion.142) | copy-start | bytes 1540
  137.3 103.0 %copy-start.7 = (f32[128,512]{1,0:T(8,128)}, f32[128,512]{1,0:T(8,128)S(1)}, u32[]{:S(2)}) copy-start(f32[128,512]{1,0:T(8,128)S(1)} %get-tuple-element.56) | copy-start | bytes 786436
  137.4 29.6 %copy-start.54 = (f32[128]{0:T(128)}, f32[128]{0:T(128)S(1)}, u32[]{:S(2)}) copy-start(f32[128]{0:T(128)S(1)} %broadcast_multiply_fusion.1) | copy-start | bytes 1540
  137.6 29.4 %copy-start.81 = (f32[128]{0:T(128)}, f32[128]{0:T(128)S(1)}, u32[]{:S(2)}) copy-start(f32[128]{0:T(128)S(1)} %multiply_reduce_fusion.6) | copy-start | bytes 1540
  137.6 29.4 %copy-start.61 = (f32[128]{0:T(128)}, f32[128]{0:T(128)S(1)}, u32[]{:S(2)}) copy-start(f32[128]{0:T(128)S(1)} %fusion.143) | copy-start | bytes 1540
  138.4 100.2 %reduce-scatter.7.cloned.1.call-start = ((), (), s32[]{:S(2)}) async-start(), calls=%async_computation.5 | async-start | bytes 589824
  138.5 50.0 %copy-start.59 = (f32[192]{0:T(256)}, f32[192]{0:T(256)S(1)}, u32[]{:S(2)}) copy-start(f32[192]{0:T(256)S(1)} %convert_element_type.148) | copy-start | bytes 2308
  138.6 65.5 %copy-start.71 = (s32[384]{0:T(512)}, s32[384]{0:T(512)S(1)}, u32[]{:S(2)}) copy-start(s32[384]{0:T(512)S(1)} %pad_add_fusion.1) | copy-start | bytes 4612
  168.5 26.5 %copy-start.9 = (f32[128,60,192]{0,2,1:T(8,128)}, f32[128,60,192]{0,2,1:T(8,128)S(1)}, u32[]{:S(2)}) copy-start(f32[128,60,192]{0,2,1:T(8,128)S(1)} %add_add_fusion.2) | copy-start | bytes 17694724
  174.9 13.6 %copy-start.2 = (f32[128,60,192]{0,2,1:T(8,128)}, f32[128,60,192]{0,2,1:T(8,128)S(1)}, u32[]{:S(2)}) copy-start(f32[128,60,192]{0,2,1:T(8,128)S(1)} %get-tuple-element.58) | copy-start | bytes 17694724
  175.0 13.6 %copy-start.29 = (f32[128,60]{0,1:T(8,128)}, f32[128,60]{0,1:T(8,128)S(1)}, u32[]{:S(2)}) copy-start(f32[128,60]{0,1:T(8,128)S(1)} %broadcast_multiply_fusion) | copy-start | bytes 92164
  177.5 11.0 %copy-start.32 = (f32[128,60]{0,1:T(8,128)}, f32[128,60]{0,1:T(8,128)S(1)}, u32[]{:S(2)}) copy-start(f32[128,60]{0,1:T(8,128)S(1)} %get-tuple-element.51) | copy-start | bytes 92164
  177.5 11.0 %copy-start.34 = (f32[128,60]{0,1:T(8,128)}, f32[128,60]{0,1:T(8,128)S(1)}, u32[]{:S(2)}) copy-start(f32[128,60]{0,1:T(8,128)S(1)} %get-tuple-element.52) | copy-start | bytes 92164
  201.7 7.3 %copy-start.16 = (bf16[128,512]{1,0:T(8,128)(2,1)S(1)}, bf16[128,512]{1,0:T(8,128)(2,1)}, u32[]{:S(2)}) copy-start(bf16[128,512]{1,0:T(8,128)(2,1)} %add_convert_fusion.4) | copy-start | bytes 393220
  207.8 129.0 %reduce-scatter.5.cloned.1.call-start = ((), (), s32[]{:S(2)}) async-start(), calls=%async_computation.3 | async-start | bytes 1179648 | tf_op jit(solution)/shard_map/reduce_scatter | solution.py:224
  209.9 28.7 %copy-start.43 = (f32[512]{0:T(512)S(1)}, f32[512]{0:T(512)}, u32[]{:S(2)}) copy-start(f32[512]{0:T(512)} %copy-done.42) | copy-start | bytes 6148
  209.9 28.7 %copy-start.55 = (f32[128]{0:T(128)S(1)}, f32[128]{0:T(128)}, u32[]{:S(2)}) copy-start(f32[128]{0:T(128)} %copy-done.54) | copy-start | bytes 1540
  209.9 28.7 %copy-start.62 = (f32[128]{0:T(128)S(1)}, f32[128]{0:T(128)}, u32[]{:S(2)}) copy-start(f32[128]{0:T(128)} %copy-done.61) | copy-start | bytes 1540
  209.9 30.4 %copy-start.82 = (f32[128]{0:T(128)S(1)}, f32[128]{0:T(128)}, u32[]{:S(2)}) copy-start(f32[128]{0:T(128)} %copy-done.81) | copy-start | bytes 1540
  216.1 27.3 %copy-start.46 = (f32[512]{0:T(512)S(1)}, f32[512]{0:T(512)}, u32[]{:S(2)}) copy-start(f32[512]{0:T(512)} %copy-done.45) | copy-start | bytes 6148
  216.2 27.3 %copy-start.58 = (f32[128]{0:T(128)S(1)}, f32[128]{0:T(128)}, u32[]{:S(2)}) copy-start(f32[128]{0:T(128)} %copy-done.57) | copy-start | bytes 1540
  216.2 27.4 %copy-start.69 = (f32[128]{0:T(128)S(1)}, f32[128]{0:T(128)}, u32[]{:S(2)}) copy-start(f32[128]{0:T(128)} %copy-done.68) | copy-start | bytes 1540
  216.2 28.8 %copy-start.80 = (f32[128]{0:T(128)S(1)}, f32[128]{0:T(128)}, u32[]{:S(2)}) copy-start(f32[128]{0:T(128)} %copy-done.79) | copy-start | bytes 1540
  245.2 8.9 %copy-start.20 = (f32[128,512]{1,0:T(8,128)}, f32[128,512]{1,0:T(8,128)S(1)}, u32[]{:S(2)}) copy-start(f32[128,512]{1,0:T(8,128)S(1)} %get-tuple-element.43) | copy-start | bytes 786436
  245.2 8.9 %copy-start.75 = (f32[128]{0:T(128)}, f32[128]{0:T(128)S(1)}, u32[]{:S(2)}) copy-start(f32[128]{0:T(128)S(1)} %negate_multiply_fusion.1) | copy-start | bytes 1540
  245.4 8.7 %copy-start.85 = (bf16[512,512]{1,0:T(8,128)(2,1)S(1)}, bf16[512,512]{1,0:T(8,128)(2,1)}, u32[]{:S(2)}) copy-start(bf16[512,512]{1,0:T(8,128)(2,1)} %param.34) | copy-start | bytes 1572868
  245.4 26.5 %slice-start = ((s8[15728640]{0:T(1024)(128)(4,1)}), s8[4194304]{0:T(1024)(128)(4,1)S(1)}, s32[]{:S(2)}) async-start(s8[15728640]{0:T(1024)(128)(4,1)} %bitcast.179), calls=%async_computation.7 | async-start | bytes 8388608
  254.1 17.8 %slice-start.1 = ((s8[15728640]{0:T(1024)(128)(4,1)}), s8[4194304]{0:T(1024)(128)(4,1)S(1)}, s32[]{:S(2)}) async-start(s8[15728640]{0:T(1024)(128)(4,1)} %bitcast.179), calls=%async_computation.8 | async-start | bytes 8388608
  254.1 17.7 %slice-start.2 = ((s8[15728640]{0:T(1024)(128)(4,1)}), s8[4194304]{0:T(1024)(128)(4,1)S(1)}, s32[]{:S(2)}) async-start(s8[15728640]{0:T(1024)(128)(4,1)} %bitcast.179), calls=%async_computation.9 | async-start | bytes 8388608
  254.1 17.7 %slice-start.3 = ((s8[15728640]{0:T(1024)(128)(4,1)}), s8[3145728]{0:T(1024)(128)(4,1)S(1)}, s32[]{:S(2)}) async-start(s8[15728640]{0:T(1024)(128)(4,1)} %bitcast.179), calls=%async_computation.10 | async-start | bytes 6291456
  254.1 17.7 %copy-start.86 = (bf16[512,512]{1,0:T(8,128)(2,1)S(1)}, bf16[512,512]{1,0:T(8,128)(2,1)}, u32[]{:S(2)}) copy-start(bf16[512,512]{1,0:T(8,128)(2,1)} %param.33) | copy-start | bytes 1572868
  287.8 6.5 %copy-start.5 = (bf16[128,60,512]{2,0,1:T(8,128)(2,1)}, bf16[128,60,512]{2,0,1:T(8,128)(2,1)S(1)}, u32[]{:S(2)}) copy-start(bf16[128,60,512]{2,0,1:T(8,128)(2,1)S(1)} %get-tuple-element.64) | copy-start | bytes 23592964
  287.9 6.5 %copy-start.25 = (s32[128,60]{0,1:T(8,128)S(1)}, s32[128,60]{0,1:T(8,128)}, u32[]{:S(2)}) copy-start(s32[128,60]{0,1:T(8,128)} %param.27) | copy-start | bytes 92164
  294.4 6.0 copy-start.53
  297.6 8.6 %copy-start.15 = (bf16[1,128,512]{2,1,0:T(8,128)(2,1)S(1)}, bf16[1,128,512]{2,1,0:T(8,128)(2,1)}, u32[]{:S(2)}) copy-start(bf16[1,128,512]{2,1,0:T(8,128)(2,1)} %param.23) | copy-start | bytes 393220
  300.4 6.2 copy-start.36
  300.4 6.4 %copy-start.22 = (f32[512,192]{0,1:T(8,128)S(1)}, f32[512,192]{0,1:T(8,128)}, u32[]{:S(2)}) copy-start(f32[512,192]{0,1:T(8,128)} %fusion.164) | copy-start | bytes 1179652
  300.4 6.4 %copy-start.39 = (f32[192,192]{0,1:T(8,128)S(1)}, f32[192,192]{0,1:T(8,128)}, u32[]{:S(2)}) copy-start(f32[192,192]{0,1:T(8,128)} %fusion.73) | copy-start | bytes 442372
  306.2 294.9 %all-reduce.4.cloned.1.call-start = ((), (), s32[]{:S(2)}) async-start(), calls=%async_computation.6 | async-start | bytes 28704768 | tf_op jit(solution)/shard_map/psum | solution.py:238
  307.9 30.1 %copy-start.31 = (f32[192,512]{1,0:T(8,128)S(1)}, f32[192,512]{1,0:T(8,128)}, u32[]{:S(2)}) copy-start(f32[192,512]{1,0:T(8,128)} %fusion.68) | copy-start | bytes 1179652
  339.8 43.5 %copy-start.17 = (bf16[1216,512]{1,0:T(8,128)(2,1)S(1)}, bf16[1216,512]{1,0:T(8,128)(2,1)}, u32[]{:S(2)}) copy-start(bf16[1216,512]{1,0:T(8,128)(2,1)} %param.32) | copy-start | bytes 3735556
  339.8 43.5 %copy-start.21 = (f32[128,512]{1,0:T(8,128)S(1)}, f32[128,512]{1,0:T(8,128)}, u32[]{:S(2)}) copy-start(f32[128,512]{1,0:T(8,128)} %copy-done.20) | copy-start | bytes 786436
  339.8 43.5 %copy-start.76 = (f32[128]{0:T(128)S(1)}, f32[128]{0:T(128)}, u32[]{:S(2)}) copy-start(f32[128]{0:T(128)} %copy-done.75) | copy-start | bytes 1540
  389.5 6.5 %copy-start.28 = (bf16[128,512]{1,0:T(8,128)(2,1)S(1)}, bf16[128,512]{1,0:T(8,128)(2,1)}, u32[]{:S(2)}) copy-start(bf16[128,512]{1,0:T(8,128)(2,1)} %reduce-scatter.5.cloned.1.call-done) | copy-start | bytes 393220
  601.1 6.0 copy-start.26
  601.1 6.9 %copy-start.11 = (f32[512,2048]{1,0:T(8,128)S(1)}, f32[512,2048]{1,0:T(8,128)}, u32[]{:S(2)}) copy-start(f32[512,2048]{1,0:T(8,128)} %get-tuple-element.74) | copy-start | bytes 12582916
  608.0 6.5 %copy-start.1 = (bf16[512,2048]{1,0:T(8,128)(2,1)S(1)}, bf16[512,2048]{1,0:T(8,128)(2,1)}, u32[]{:S(2)}) copy-start(bf16[512,2048]{1,0:T(8,128)(2,1)} %param.37) | copy-start | bytes 6291460
  (38 other events, 149.2 us)
Sparse Core Ops, SparseCore 0:
  9.6 24.7 all-gather.6
  138.5 20.3 all-gather.4
  207.9 30.6 reduce-scatter.6
  306.3 30.3 reduce-scatter.4
  345.3 255.7 all-reduce.3
where the time goes:
time: 629 us; the launch traced here: 621 us
  waiting for transfers between devices  263 us (42%)
  matrix products  202 us (32%)
  local copies, waits for them, and re-layouts  66.6 us (11%)
  blocking collectives  53.5 us (9%)
  other arithmetic  20.6 us (3%)
  between operations  15.6 us (2%)
    psum x1, waiting for transfers between devices, local(): lax.psum((grad_message_in, grad_message_mid, grad_message_out, grad_gain_...  204 us
    dot_general x6, matrix products, edge_input_grad(): jnp.einsum('rkf,ef->rke', grads, weight, preferred_element_type=jnp.float32)  57 us
    gather x2, local copies, waits for them, and re-layouts, local(): other_tag = jnp.take(table_tags, neighbour, axis=0)  45.3 us
    psum x1, blocking collectives, local(): lax.psum((grad_message_in, grad_message_mid, grad_message_out, grad_gain_...  40.1 us
    dot_general x6, matrix products, edge_weight_grad(): jnp.einsum('rke,rkf->ef', edges, grads, preferred_element_type=jnp.float32)  39.7 us
    dot_general x6, matrix products, edge_dot(): jnp.einsum('rke,ef->rkf', edges, weight, preferred_element_type=jnp.float32)  38.1 us
    unnamed x6, waiting for transfers between devices  23.2 us
    dot_general x2, matrix products, pick_rows(): jnp.einsum('rkl,ld->rkd', picker, upper, preferred_element_type=jnp.float32)  20.2 us
  transfers between devices with their start and end apart: 5, of which 4 were waited for; matrix products, arithmetic and copies ran while one was open for 17% of the time, Pallas kernels for 0%

commit v1 on v0

--- a/solution.py
+++ b/solution.py
@@ -235,25 +235,24 @@
     grad_update_in = jnp.concatenate(
         [grad_update_self, grad_update_neigh, grad_update_edge], axis=0
     )
-    totals = lax.psum(
-        (
-            grad_message_in,
-            grad_message_mid,
-            grad_message_out,
-            grad_gain_node,
-            grad_offset_node,
-            grad_expand,
-            grad_contract,
-            grad_gain_ffn,
-            grad_offset_ffn,
-            grad_update_in,
-            grad_update_mid,
-            grad_update_out,
-            grad_gain_edge,
-            grad_offset_edge,
-        ),
-        ("tm", "res"),
-    )
+    totals = (
+        grad_message_in,
+        grad_message_mid,
+        grad_message_out,
+        grad_gain_node,
+        grad_offset_node,
+        grad_expand,
+        grad_contract,
+        grad_gain_ffn,
+        grad_offset_ffn,
+        grad_update_in,
+        grad_update_mid,
+        grad_update_out,
+        grad_gain_edge,
+        grad_offset_edge,
+    )
+    for axis in ("res", "tm"):
+        totals = lax.psum(totals, axis)
     return (
         updated_low[None],
         edge_new.astype(jnp.bfloat16)[None],

time: 629 us -> 938 us (1.49)
  waiting for transfers between devices: 263 us -> 566 us
    psum x1 -> x2, waiting for transfers between devices: 204 us -> 507 us  [local(): totals = lax.psum(totals, axis)]
    psum x1 -> x2, blocking collectives: 40.1 us -> 45.3 us  [local(): totals = lax.psum(totals, axis)]
    unnamed x6 -> x7, waiting for transfers between devices: 23.2 us -> 23.2 us
  transfers between devices with their start and end apart: 5 -> 6, of which waited for: 4 -> 5; matrix products, arithmetic and copies ran while one was open for 17% -> 11% of each run, Pallas kernels for 0% -> 0%
where the time goes in v1:
time: 938 us; the launch traced here: 930 us
  waiting for transfers between devices  566 us (60%)
  matrix products  202 us (22%)
  local copies, waits for them, and re-layouts  66.1 us (7%)
  blocking collectives  58.7 us (6%)
  other arithmetic  20.6 us (2%)
  between operations  16 us (2%)
    psum x2, waiting for transfers between devices, local(): totals = lax.psum(totals, axis)  507 us
    dot_general x6, matrix products, edge_input_grad(): jnp.einsum('rkf,ef->rke', grads, weight, preferred_element_type=jnp.float32)  57.2 us
    gather x2, local copies, waits for them, and re-layouts, local(): other_tag = jnp.take(table_tags, neighbour, axis=0)  45.3 us
    psum x2, blocking collectives, local(): totals = lax.psum(totals, axis)  45.3 us
    dot_general x6, matrix products, edge_weight_grad(): jnp.einsum('rke,rkf->ef', edges, grads, preferred_element_type=jnp.float32)  39.7 us
    dot_general x6, matrix products, edge_dot(): jnp.einsum('rke,ef->rkf', edges, weight, preferred_element_type=jnp.float32)  38.1 us
    unnamed x7, waiting for transfers between devices  23.2 us
    dot_general x2, matrix products, pick_rows(): jnp.einsum('rkl,ld->rkd', picker, upper, preferred_element_type=jnp.float32)  20.2 us
  transfers between devices with their start and end apart: 6, of which 5 were waited for; matrix products, arithmetic and copies ran while one was open for 11% of the time, Pallas kernels for 0%

profile of v1, /device:TPU:0, one launch (start us, length us, event | category | flops | bytes accessed | tf_op | source)
XLA Modules:
  0.0 929.9 jit_solution(4560519678609903173)
XLA Ops:
  13.0 13.4 %all-gather.1 = s32[8,1,128]{2,1,0:T(1,128)S(1)} all-gather(s32[1,1,128]{2,1,0:T(1,128)S(1)} %bitcast.183), channel_id=1, replica_groups=mesh['tm'=4,'res'=8] {'res'}, dimensions={0}, use_global_device_ids=true | all-gather | bytes 4608 | tf_op jit(solution)/shard_map/all_gather | solution.py:121
  27.3 1.4 gather_fusion
  28.8 45.2 %gather_fusion.1 = s32[7680]{0:T(1024)S(1)} fusion(s32[384]{0:T(512)S(1)} %pad_add_fusion, s32[8192]{0:T(1024)S(1)} %pad_clamp_fusion), kind=kCustom, calls=%fused_computation.1 | custom fusion | bytes 92160 | tf_op jit(solution)/shard_map/jit(_take)/gather | solution.py:128
  74.6 1.3 fusion.97
  75.8 9.6 %fusion.58 = f32[128,60,512]{2,0,1:T(8,128)} fusion(bf16[1,128,60,192]{1,3,2,0:T(8,128)(2,1)} %param.24, bf16[1216,512]{1,0:T(8,128)(2,1)} %param.32), kind=kOutput, calls=%fused_computation.85 | convolution fusion | flops 1509949440 | bytes 18874368 | tf_op jit(solution)/shard_map/rke,ef->rkf/dot_general | solution.py:36
  85.4 1.7 convolution_convert_fusion.1
  87.2 1.4 fusion.94
  88.6 7.7 fusion.18
  96.3 17.7 %add_add_fusion = f32[128,60,512]{2,0,1:T(8,128)} fusion(f32[128,60,512]{2,0,1:T(8,128)} %fusion.58, f32[128,60,512]{2,0,1:T(8,128)} %fusion.18, f32[128,512]{1,0:T(8,128)S(1)} %fusion.97, s32[128,60]{0,1:T(8,128)S(1)} %copy-done.24, f32[384,512]{1,0:T(8,128)S(1)} %fusion.94), kind=kOutput, calls=%fused_computation.24 | convolution fusion | flops 3034841088 | bytes 48265216 | tf_op jit(solution)/shard_map/rkl,ld->rkd/dot_general | solution.py:61
  114.0 16.2 %multiply_convert_fusion.1 = (bf16[128,60,512]{2,0,1:T(8,128)(2,1)S(1)}, f32[128,60,512]{2,0,1:T(8,128)}) fusion(bf16[512,512]{1,0:T(8,128)(2,1)} %param.33, f32[128,60,512]{2,0,1:T(8,128)} %add_add_fusion), kind=kOutput, calls=%fused_computation.22 | convolution fusion | flops 4097310720 | bytes 39845888 | tf_op jit(solution)/shard_map/rke,ef->rkf/dot_general | solution.py:36
  130.2 4.5 multiply_reduce_fusion
  135.7 1.0 copy-done.12
  138.6 1.1 fusion.118
  139.7 19.2 %all-gather.5.cloned.1.call-done = bf16[1024,512]{1,0:T(8,128)(2,1)} async-done(((bf16[128,512]{1,0:T(8,128)(2,1)}), bf16[1024,512]{1,0:T(8,128)(2,1)}) %all-gather.5.cloned.1.call-update) | async-done | bytes 1048592 | tf_op jit(solution)/shard_map/all_gather | solution.py:158
  158.9 1.7 convolution_convert_fusion
  160.6 1.2 fusion.104
  161.8 2.7 fusion.16
  164.5 2.4 fusion.17
  167.0 1.5 add_add_fusion.2
  168.5 3.3 fusion.128
  171.9 3.1 fusion.161
  175.0 2.5 fusion.29
  177.6 6.6 fusion.30
  184.2 4.3 convolution_bitcast_fusion.3
  188.6 6.4 fusion.44
  195.0 5.0 fusion.162
  200.0 1.6 fusion.73
  201.7 2.3 fusion.71
  204.0 1.7 fusion.67
  205.8 2.0 copy.84
  207.8 1.1 convolution_add_fusion.4
  209.0 0.9 fusion.164
  209.9 6.2 convolution_bitcast_fusion.4
  216.2 22.4 %reduce-scatter.7.cloned.1.call-done = bf16[128,192]{1,0:T(8,128)(2,1)} async-done(((bf16[1024,192]{1,0:T(8,128)(2,1)}), bf16[128,192]{1,0:T(8,128)(2,1)}) %reduce-scatter.7.cloned.1.call-update) | async-done | bytes 49168
  238.6 1.7 multiply_reduce_fusion.2
  240.6 2.9 fusion.82
  243.5 1.5 multiply_reduce_fusion.3
  245.4 8.7 fusion.65
  254.1 17.7 %fusion.13 = bf16[128,60,512]{2,0,1:T(8,128)(2,1)} fusion(f32[128,60,512]{2,0,1:T(8,128)} %get-tuple-element.68, f32[128,512]{1,0:T(8,128)S(1)} %add_divide_fusion, f32[128,60]{0,1:T(8,128)S(1)} %copy-done.49, bf16[512,512]{1,0:T(8,128)(2,1)S(1)} %copy-done.85), kind=kOutput, calls=%fused_computation.19 | convolution fusion | flops 4113039360 | bytes 24410112 | tf_op jit(solution)/shard_map/rkf,ef->rke/dot_general | solution.py:44
  271.9 15.9 %fusion.163 = (bf16[128,512]{1,0:T(8,128)(2,1)S(1)}, bf16[128,60,512]{2,0,1:T(8,128)(2,1)S(1)}) fusion(f32[128,60,512]{2,0,1:T(8,128)S(1)} %bitcast.180, bf16[128,60,512]{2,0,1:T(8,128)(2,1)} %fusion.13, bf16[512,512]{1,0:T(8,128)(2,1)S(1)} %copy-done.86), kind=kOutput, calls=%fused_computation.246 | convolution fusion | flops 4109041664 | bytes 32112640 | tf_op jit(solution)/shard_map/rkf,ef->rke/dot_general | solution.py:44
  287.8 6.5 fusion.68
  294.4 3.2 fusion.66
  297.6 2.8 fusion.149
  300.4 2.8 fusion.151
  303.3 2.9 fusion.64
  306.8 1.0 pad_maximum_fusion.1
  307.8 12.3 %convolution_bitcast_fusion = f32[512,512]{1,0:T(8,128)} fusion(bf16[128,60,512]{2,0,1:T(8,128)(2,1)} %fusion.13, f32[128,60,512]{2,0,1:T(8,128)} %add_add_fusion), kind=kOutput, calls=%fused_computation.95 | convolution fusion | flops 4061921280 | bytes 24641536 | tf_op jit(solution)/shard_map/rke,rkf->ef/dot_general | solution.py:40
  320.2 16.6 %reduce-scatter.5.cloned.1.call-done = bf16[128,512]{1,0:T(8,128)(2,1)} async-done(((bf16[1024,512]{1,0:T(8,128)(2,1)}), bf16[128,512]{1,0:T(8,128)(2,1)}) %reduce-scatter.5.cloned.1.call-update) | async-done | bytes 131088 | tf_op jit(solution)/shard_map/reduce_scatter | solution.py:224
  336.7 1.2 convolution_bitcast_fusion.1
  338.0 1.7 pad_maximum_fusion
  339.7 290.1 %all-reduce.7.cloned.1.call-done = (f32[1216,512]{1,0:T(8,128)}, f32[512,512]{1,0:T(8,128)}, f32[512,512]{1,0:T(8,128)}, f32[512,2048]{1,0:T(8,128)}, f32[2048,5...) async-done(((f32[1216,512]{1,0:T(8,128)}, f32[512,512]{1,0:T(8,128)}, f32[512,512]{1,0:T(8,128)}, f32[512,2048]{1,0:T(8,128)}, ...) | async-done | bytes 14204944 | tf_op jit(solution)/shard_map/psum | solution.py:255
  630.0 2.5 convert_reduce_fusion
  633.3 28.0 %all-reduce = (f32[512]{0:T(512)S(1)}, f32[512]{0:T(512)S(1)}, f32[512]{0:T(512)S(1)}, f32[512]{0:T(512)S(1)}, f32[192]{0:T(256)S(1)}, /*index=5*/f32[192]{0:T(256)S(1)}) all-reduce(f32[512]{0:T(512)S(1)} %copy-done.66, f32[512]{0:T(512)S(1)} %copy-done.67, f32[512]{0:T(512)S(1)} %copy-done.64, ...), channel_id=1, replica_groups=mesh['tm'=4,'res'=8] {'res'}, use_global_device_ids=true, to_apply=%region_25.26 | all-reduce | flops 2432 | bytes 19456 | tf_op jit(solution)/shard_map/psum | solution.py:255
  661.3 17.4 %all-reduce.2 = (f32[512]{0:T(512)}, f32[512]{0:T(512)}, f32[512]{0:T(512)}, f32[512]{0:T(512)}, f32[192]{0:T(256)}, /*index=5*/f32[192]{0:T(256)}) all-reduce(f32[512]{0:T(512)S(1)} %get-tuple-element.28, f32[512]{0:T(512)S(1)} %get-tuple-element.29, f32[512]{0:T(512)S(1)} %get-tuple-element.30, ...), channel_id=1, replica_groups=mesh['tm'=4,'res'=8] {'tm'}, use_global_device_ids=true, to_apply=%region_26.27 | all-reduce | flops 2432 | bytes 19456 | tf_op jit(solution)/shard_map/psum | solution.py:255
  679.0 5.5 fusion.110
  684.7 6.6 add_bitcast_fusion
  691.3 1.0 fusion.72
  692.3 216.9 %all-reduce.9.cloned.1.call-done = (f32[1216,512]{1,0:T(8,128)}, f32[512,512]{1,0:T(8,128)}, f32[512,512]{1,0:T(8,128)}, f32[512,2048]{1,0:T(8,128)}, f32[2048,5...) async-done(((f32[1216,512]{1,0:T(8,128)}, f32[512,512]{1,0:T(8,128)}, f32[512,512]{1,0:T(8,128)}, f32[512,2048]{1,0:T(8,128)}, ...) | async-done | bytes 14204944 | tf_op jit(solution)/shard_map/psum | solution.py:255
  909.3 3.5 copy.102
  912.8 2.4 copy.103
  915.2 1.0 copy.104
  916.2 2.1 copy.105
  918.3 2.0 copy.106
  920.3 0.9 copy.107
  (257 shorter events, 13.9 us)
Async XLA Ops:
  7.2 128.0 %copy-start = (bf16[512,2048]{1,0:T(8,128)(2,1)S(1)}, bf16[512,2048]{1,0:T(8,128)(2,1)}, u32[]{:S(2)}) copy-start(bf16[512,2048]{1,0:T(8,128)(2,1)} %param.37) | copy-start | bytes 6291460
  7.2 78.2 %all-gather.7.cloned.1.call-start = ((), (), s32[]{:S(2)}) async-start(), calls=%async_computation.4 | async-start | bytes 1179648 | tf_op jit(solution)/shard_map/all_gather | solution.py:120
  7.9 150.9 %all-gather.5.cloned.1.call-start = ((), (), s32[]{:S(2)}) async-start(), calls=%async_computation.2 | async-start | bytes 1179648 | tf_op jit(solution)/shard_map/all_gather | solution.py:158
  10.2 125.5 %copy-start.45 = (f32[512]{0:T(512)}, f32[512]{0:T(512)S(1)}, u32[]{:S(2)}) copy-start(f32[512]{0:T(512)S(1)} %convert_element_type.134) | copy-start | bytes 6148
  10.9 126.7 %copy-start.42 = (f32[512]{0:T(512)}, f32[512]{0:T(512)S(1)}, u32[]{:S(2)}) copy-start(f32[512]{0:T(512)S(1)} %convert_element_type.138) | copy-start | bytes 6148
  11.6 124.1 %copy-start.52 = (f32[512]{0:T(512)}, f32[512]{0:T(512)S(1)}, u32[]{:S(2)}) copy-start(f32[512]{0:T(512)S(1)} %convert_element_type.135) | copy-start | bytes 6148
  12.3 125.3 %copy-start.50 = (f32[512]{0:T(512)}, f32[512]{0:T(512)S(1)}, u32[]{:S(2)}) copy-start(f32[512]{0:T(512)S(1)} %convert_element_type.139) | copy-start | bytes 6148
  28.7 45.4 %copy-start.47 = (s32[128,60]{0,1:T(8,128)S(1)}, s32[128,60]{0,1:T(8,128)}, u32[]{:S(2)}) copy-start(s32[128,60]{0,1:T(8,128)} %param.28) | copy-start | bytes 92164
  28.7 45.5 %copy-start.77 = (s32[128]{0:T(128)S(1)}, s32[128]{0:T(128)}, u32[]{:S(2)}) copy-start(s32[128]{0:T(128)} %param.31) | copy-start | bytes 1540
  28.7 45.5 %copy-start.78 = (s32[128]{0:T(128)S(1)}, s32[128]{0:T(128)}, u32[]{:S(2)}) copy-start(s32[128]{0:T(128)} %param.30) | copy-start | bytes 1540
  28.8 45.8 %copy-start.14 = (bf16[1,128,512]{2,1,0:T(8,128)(2,1)S(1)}, bf16[1,128,512]{2,1,0:T(8,128)(2,1)}, u32[]{:S(2)}) copy-start(bf16[1,128,512]{2,1,0:T(8,128)(2,1)} %param.23) | copy-start | bytes 393220
  74.5 55.7 %copy-start.48 = (f32[128,60]{0,1:T(8,128)}, f32[128,60]{0,1:T(8,128)S(1)}, u32[]{:S(2)}) copy-start(f32[128,60]{0,1:T(8,128)S(1)} %copy.62) | copy-start | bytes 92164
  74.6 60.2 %copy-start.73 = (f32[128]{0:T(128)}, f32[128]{0:T(128)S(1)}, u32[]{:S(2)}) copy-start(f32[128]{0:T(128)S(1)} %broadcast_maximum_fusion) | copy-start | bytes 1540
  75.8 12.7 %copy-start.24 = (s32[128,60]{0,1:T(8,128)S(1)}, s32[128,60]{0,1:T(8,128)}, u32[]{:S(2)}) copy-start(s32[128,60]{0,1:T(8,128)} %param.27) | copy-start | bytes 92164
  114.0 16.2 %copy-start.84 = (bf16[512,512]{1,0:T(8,128)(2,1)S(1)}, bf16[512,512]{1,0:T(8,128)(2,1)}, u32[]{:S(2)}) copy-start(bf16[512,512]{1,0:T(8,128)(2,1)} %param.34) | copy-start | bytes 1572868
  130.2 6.5 copy-start.83
  135.2 26.7 %copy-start.79 = (f32[128]{0:T(128)}, f32[128]{0:T(128)S(1)}, u32[]{:S(2)}) copy-start(f32[128]{0:T(128)S(1)} %multiply_reduce_fusion.7) | copy-start | bytes 1540
  135.2 26.6 %copy-start.68 = (f32[128]{0:T(128)}, f32[128]{0:T(128)S(1)}, u32[]{:S(2)}) copy-start(f32[128]{0:T(128)S(1)} %fusion.142) | copy-start | bytes 1540
  137.3 103.0 %copy-start.7 = (f32[128,512]{1,0:T(8,128)}, f32[128,512]{1,0:T(8,128)S(1)}, u32[]{:S(2)}) copy-start(f32[128,512]{1,0:T(8,128)S(1)} %get-tuple-element.70) | copy-start | bytes 786436
  137.4 29.6 %copy-start.54 = (f32[128]{0:T(128)}, f32[128]{0:T(128)S(1)}, u32[]{:S(2)}) copy-start(f32[128]{0:T(128)S(1)} %broadcast_multiply_fusion.1) | copy-start | bytes 1540
  137.6 29.4 %copy-start.81 = (f32[128]{0:T(128)}, f32[128]{0:T(128)S(1)}, u32[]{:S(2)}) copy-start(f32[128]{0:T(128)S(1)} %multiply_reduce_fusion.6) | copy-start | bytes 1540
  137.6 29.4 %copy-start.61 = (f32[128]{0:T(128)}, f32[128]{0:T(128)S(1)}, u32[]{:S(2)}) copy-start(f32[128]{0:T(128)S(1)} %fusion.143) | copy-start | bytes 1540
  138.4 100.2 %reduce-scatter.7.cloned.1.call-start = ((), (), s32[]{:S(2)}) async-start(), calls=%async_computation.5 | async-start | bytes 589824
  138.5 50.0 %copy-start.59 = (f32[192]{0:T(256)}, f32[192]{0:T(256)S(1)}, u32[]{:S(2)}) copy-start(f32[192]{0:T(256)S(1)} %convert_element_type.148) | copy-start | bytes 2308
  138.6 65.5 %copy-start.71 = (s32[384]{0:T(512)}, s32[384]{0:T(512)S(1)}, u32[]{:S(2)}) copy-start(s32[384]{0:T(512)S(1)} %pad_add_fusion.1) | copy-start | bytes 4612
  168.5 26.5 %copy-start.9 = (f32[128,60,192]{0,2,1:T(8,128)}, f32[128,60,192]{0,2,1:T(8,128)S(1)}, u32[]{:S(2)}) copy-start(f32[128,60,192]{0,2,1:T(8,128)S(1)} %add_add_fusion.2) | copy-start | bytes 17694724
  174.9 13.6 %copy-start.2 = (f32[128,60,192]{0,2,1:T(8,128)}, f32[128,60,192]{0,2,1:T(8,128)S(1)}, u32[]{:S(2)}) copy-start(f32[128,60,192]{0,2,1:T(8,128)S(1)} %get-tuple-element.72) | copy-start | bytes 17694724
  175.0 13.6 %copy-start.29 = (f32[128,60]{0,1:T(8,128)}, f32[128,60]{0,1:T(8,128)S(1)}, u32[]{:S(2)}) copy-start(f32[128,60]{0,1:T(8,128)S(1)} %broadcast_multiply_fusion) | copy-start | bytes 92164
  177.5 11.0 %copy-start.32 = (f32[128,60]{0,1:T(8,128)}, f32[128,60]{0,1:T(8,128)S(1)}, u32[]{:S(2)}) copy-start(f32[128,60]{0,1:T(8,128)S(1)} %get-tuple-element.65) | copy-start | bytes 92164
  177.5 11.0 %copy-start.34 = (f32[128,60]{0,1:T(8,128)}, f32[128,60]{0,1:T(8,128)S(1)}, u32[]{:S(2)}) copy-start(f32[128,60]{0,1:T(8,128)S(1)} %get-tuple-element.66) | copy-start | bytes 92164
  201.7 7.3 copy-start.16
  207.8 128.9 %reduce-scatter.5.cloned.1.call-start = ((), (), s32[]{:S(2)}) async-start(), calls=%async_computation.3 | async-start | bytes 1179648 | tf_op jit(solution)/shard_map/reduce_scatter | solution.py:224
  209.9 28.7 %copy-start.43 = (f32[512]{0:T(512)S(1)}, f32[512]{0:T(512)}, u32[]{:S(2)}) copy-start(f32[512]{0:T(512)} %copy-done.42) | copy-start | bytes 6148
  209.9 28.7 %copy-start.55 = (f32[128]{0:T(128)S(1)}, f32[128]{0:T(128)}, u32[]{:S(2)}) copy-start(f32[128]{0:T(128)} %copy-done.54) | copy-start | bytes 1540
  209.9 28.7 %copy-start.62 = (f32[128]{0:T(128)S(1)}, f32[128]{0:T(128)}, u32[]{:S(2)}) copy-start(f32[128]{0:T(128)} %copy-done.61) | copy-start | bytes 1540
  209.9 30.4 %copy-start.82 = (f32[128]{0:T(128)S(1)}, f32[128]{0:T(128)}, u32[]{:S(2)}) copy-start(f32[128]{0:T(128)} %copy-done.81) | copy-start | bytes 1540
  216.1 27.4 %copy-start.46 = (f32[512]{0:T(512)S(1)}, f32[512]{0:T(512)}, u32[]{:S(2)}) copy-start(f32[512]{0:T(512)} %copy-done.45) | copy-start | bytes 6148
  216.2 27.4 %copy-start.58 = (f32[128]{0:T(128)S(1)}, f32[128]{0:T(128)}, u32[]{:S(2)}) copy-start(f32[128]{0:T(128)} %copy-done.57) | copy-start | bytes 1540
  216.2 27.4 %copy-start.69 = (f32[128]{0:T(128)S(1)}, f32[128]{0:T(128)}, u32[]{:S(2)}) copy-start(f32[128]{0:T(128)} %copy-done.68) | copy-start | bytes 1540
  216.2 28.8 %copy-start.80 = (f32[128]{0:T(128)S(1)}, f32[128]{0:T(128)}, u32[]{:S(2)}) copy-start(f32[128]{0:T(128)} %copy-done.79) | copy-start | bytes 1540
  245.2 8.9 copy-start.20
  245.2 8.9 copy-start.75
  245.4 8.7 copy-start.85
  245.4 26.4 %slice-start = ((s8[15728640]{0:T(1024)(128)(4,1)}), s8[4194304]{0:T(1024)(128)(4,1)S(1)}, s32[]{:S(2)}) async-start(s8[15728640]{0:T(1024)(128)(4,1)} %bitcast.179), calls=%async_computation.8 | async-start | bytes 8388608
  254.1 17.7 %slice-start.1 = ((s8[15728640]{0:T(1024)(128)(4,1)}), s8[4194304]{0:T(1024)(128)(4,1)S(1)}, s32[]{:S(2)}) async-start(s8[15728640]{0:T(1024)(128)(4,1)} %bitcast.179), calls=%async_computation.9 | async-start | bytes 8388608
  254.1 17.7 %slice-start.2 = ((s8[15728640]{0:T(1024)(128)(4,1)}), s8[4194304]{0:T(1024)(128)(4,1)S(1)}, s32[]{:S(2)}) async-start(s8[15728640]{0:T(1024)(128)(4,1)} %bitcast.179), calls=%async_computation.10 | async-start | bytes 8388608
  254.1 17.7 %slice-start.3 = ((s8[15728640]{0:T(1024)(128)(4,1)}), s8[3145728]{0:T(1024)(128)(4,1)S(1)}, s32[]{:S(2)}) async-start(s8[15728640]{0:T(1024)(128)(4,1)} %bitcast.179), calls=%async_computation.11 | async-start | bytes 6291456
  254.1 17.7 %copy-start.86 = (bf16[512,512]{1,0:T(8,128)(2,1)S(1)}, bf16[512,512]{1,0:T(8,128)(2,1)}, u32[]{:S(2)}) copy-start(bf16[512,512]{1,0:T(8,128)(2,1)} %param.33) | copy-start | bytes 1572868
  287.8 6.5 copy-start.5
  287.8 6.5 copy-start.25
  294.4 6.0 copy-start.53
  297.6 8.6 copy-start.15
  300.4 6.2 copy-start.36
  300.4 6.4 copy-start.22
  300.4 6.4 copy-start.39
  306.2 323.7 %all-reduce.7.cloned.1.call-start = ((), (), s32[]{:S(2)}) async-start(), calls=%async_computation.6 | async-start | bytes 28704768 | tf_op jit(solution)/shard_map/psum | solution.py:255
  307.8 30.1 %copy-start.31 = (f32[192,512]{1,0:T(8,128)S(1)}, f32[192,512]{1,0:T(8,128)}, u32[]{:S(2)}) copy-start(f32[192,512]{1,0:T(8,128)} %fusion.68) | copy-start | bytes 1179652
  339.7 569.6 %all-reduce.9.cloned.1.call-start = ((), (), s32[]{:S(2)}) async-start(), calls=%async_computation.7 | async-start | bytes 28704768 | tf_op jit(solution)/shard_map/psum | solution.py:255
  630.0 48.7 %copy-start.17 = (bf16[1216,512]{1,0:T(8,128)(2,1)S(1)}, bf16[1216,512]{1,0:T(8,128)(2,1)}, u32[]{:S(2)}) copy-start(bf16[1216,512]{1,0:T(8,128)(2,1)} %param.32) | copy-start | bytes 3735556
  630.0 48.7 %copy-start.21 = (f32[128,512]{1,0:T(8,128)S(1)}, f32[128,512]{1,0:T(8,128)}, u32[]{:S(2)}) copy-start(f32[128,512]{1,0:T(8,128)} %copy-done.20) | copy-start | bytes 786436
  630.0 48.7 %copy-start.76 = (f32[128]{0:T(128)S(1)}, f32[128]{0:T(128)}, u32[]{:S(2)}) copy-start(f32[128]{0:T(128)} %copy-done.75) | copy-start | bytes 1540
  684.7 6.7 copy-start.28
  909.2 6.9 copy-start.11
  916.2 6.5 copy-start.1
  (39 other events, 153.8 us)
Sparse Core Ops, SparseCore 0:
  9.6 24.7 all-gather.6
  138.5 20.3 all-gather.4
  207.9 30.6 reduce-scatter.6
  306.3 30.3 reduce-scatter.4
  341.0 288.8 all-reduce.6
  635.1 274.1 all-reduce.8
